TPU v7x, 256 devices: a whole 4x4x8 slice. The times are simulated.
256 devices in a mesh: row: 32 (over y, x, core), col: 8 (over z).
Axes of the slice: x: 4, y: 4, z: 8, core: 2. Of those that a mesh axis runs over, the one named last changes fastest.
Arguments:
- head_points: float32 [8, 2, 1024], P(None, None, 'row'), may hold values from 0 to 1
- tail_points: float32 [8, 32768], P(None, 'row'), may hold values from 0 to 1
- eval_points: float32 [8, 8192], P(None, 'col'), may hold values from 0 to 1
- length_scales: float32 [8], replicated, may hold values from 0.5 to 2
- head_factor: float32 [2, 1024, 2, 1024], P(None, 'row', None, 'col'), as said below
- tail_factor: float32 [32768, 2, 1024], P('row', None, 'col'), may hold values from -0.125 to 0.125
Outputs:
- head_solved: float32 [2, 1024, 8192], P(None, 'row', 'col')
- tail_rhs: float32 [32768, 8192], P('row', 'col')
Inputs may be any that keep to these rules, and one draw needn't show every extreme that they name: head_factor[p, :, q, :] is zero for q > p; the blocks with p = q are lower triangular with a diagonal between 1 and 2.
All inputs are finite; a program needn't handle non-finite values.
Results may differ from a plain program's by a relative error of at most 0.00011.
Values sent between devices are 32-bit elements; how exact they have to be, the bound alone decides.
No kernel may reach another device: no remote copies, remote signals or barrier semaphores. Data moves between devices by JAX's collectives and lax.ppermute only.
A program may use at most 192 MiB of HBM per device.

v0:
```python
import jax
import jax.numpy as jnp
from jax import lax
from jax.sharding import PartitionSpec as P


def kernel_block(row_points, col_points, length_scales):
    total = jnp.zeros((row_points.shape[1], col_points.shape[1]), jnp.float32)
    for dimension in range(row_points.shape[0]):
        spread = (row_points[dimension][:, None] - col_points[dimension][None, :]) / length_scales[
            dimension
        ]
        total = total + spread * spread
    scaled = jnp.sqrt(5.0 * total)
    return (1.0 + scaled + scaled * scaled / 3.0) * jnp.exp(-scaled)


def whole_triangle(block):
    band = lax.all_gather(block, "col", axis=1, tiled=True)
    return lax.all_gather(band, "row", axis=0, tiled=True)


def solve_panel(block, right_side):
    triangle = whole_triangle(block)
    spread = lax.all_to_all(right_side, "row", split_axis=1, concat_axis=0, tiled=True)
    partial_value = jax.scipy.linalg.solve_triangular(triangle, spread, lower=True)
    return lax.all_gather(partial_value, "row", axis=1, tiled=True)


def apply_panel(rows_factor, solved):
    return jnp.dot(
        lax.all_gather(rows_factor, "col", axis=1, tiled=True),
        solved,
        precision=lax.Precision.HIGHEST,
        preferred_element_type=jnp.float32,
    )


def per_device(head_points, tail_points, eval_points, length_scales, head_factor, tail_factor):
    panel_rows = head_factor.shape[1]
    row_index = lax.axis_index("row")
    second = kernel_block(head_points[:, 1, :], eval_points, length_scales)
    tail = kernel_block(tail_points, eval_points, length_scales)
    first = kernel_block(head_points[:, 0, :], eval_points, length_scales)
    solved_one = solve_panel(head_factor[0, :, 0, :], first)
    update_rows = jnp.concatenate([head_factor[1, :, 0, :], tail_factor[:, 0, :]], 0)
    change = apply_panel(update_rows, solved_one)
    second_rhs = second - change[:panel_rows]
    tail = tail - change[panel_rows:]
    solved_two = solve_panel(head_factor[1, :, 1, :], second_rhs)
    tail = tail - apply_panel(tail_factor[:, 1, :], solved_two)
    local_one = lax.dynamic_slice_in_dim(solved_one, row_index * panel_rows, panel_rows, 0)
    local_two = lax.dynamic_slice_in_dim(solved_two, row_index * panel_rows, panel_rows, 0)
    return (jnp.stack([local_one, local_two]), tail)


def solution(mesh):
    placed = (
        P(None, None, "row"),
        P(None, "row"),
        P(None, "col"),
        P(),
        P(None, "row", None, "col"),
        P("row", None, "col"),
    )
    return jax.shard_map(
        per_device,
        mesh=mesh,
        in_specs=placed,
        out_specs=(P(None, "row", "col"), P("row", "col")),
        check_vma=False,
    )
```

profile of v0, /device:TPU:0, one launch (start us, length us, event | category | flops | bytes accessed | tf_op | source)
XLA Modules:
  0.0 561.0 jit_solution(13465957353782075579)
XLA Ops:
  8.1 28.5 %all-gather = f32[1,32,1,1024]{3,1,2,0:T(8,128)} all-gather(f32[1,32,1,128]{3,1,2,0:T(8,128)S(1)} %bitcast.220), channel_id=2, replica_groups=mesh['row'=32,'col'=8] {'col'}, dimensions={3}, use_global_device_ids=true | all-gather | bytes 147456 | tf_op jit(solution)/shard_map/all_gather | solution.py:19
  36.7 26.6 %all-gather.2 = f32[1,32,1,1024]{3,1,2,0:T(8,128)} all-gather(f32[1,32,1,128]{3,1,2,0:T(8,128)S(1)} %bitcast.219), channel_id=4, replica_groups=mesh['row'=32,'col'=8] {'col'}, dimensions={3}, use_global_device_ids=true | all-gather | bytes 147456 | tf_op jit(solution)/shard_map/all_gather | solution.py:19
  63.3 3.3 fusion.73
  68.9 6.2 %fusion.77 = f32[32,32,32]{2,1,0:T(8,128)S(1)} fusion(f32[]{:T(128)} %bitcast.17, f32[32,32]{1,0:T(8,128)S(1)} %sub.446, f32[32]{0:T(128)S(1)} %get-tuple-element.124, f32[]{:T(128)} %bitcast.15, f32[32,32]{1,0:T(8,128)S(1)} %sub.441, f32[32]{0:T(128)S(1)} %get-tuple-element.125, f32[]{:T(128)} %bitcast.13, f32[32,32]{1,0:T(8,128)S(1)} %sub.436, ...), kind=kLoop, calls=%fused_computation.196 | loop fusion | flops 1245184 | bytes 164896
  76.0 7.3 %all-to-all-start = ((f32[32,1,1024]{2,1,0:T(1,128)}), f32[32,1,1024]{2,1,0:T(1,128)S(1)}, u32[]{:S(2)}, u32[]{:S(2)}) async-start(f32[32,1,1024]{2,1,0:T(1,128)} %reshape.231), calls=%async_computation | async-start | bytes 262144 | tf_op jit(solution)/shard_map/all_to_all | solution.py:25
  83.4 7.7 %all-to-all-done = f32[32,1,1024]{2,1,0:T(1,128)S(1)} async-done(((f32[32,1,1024]{2,1,0:T(1,128)}), f32[32,1,1024]{2,1,0:T(1,128)S(1)}, u32[]{:S(2)}, u32[]{:S(2)}) %all-to-all-start) | async-done | bytes 131104 | tf_op jit(solution)/shard_map/all_to_all | solution.py:25
  93.5 4.8 bitcast_select_fusion.1
  98.3 24.1 %while.4 = (s32[]{:T(128)}, f32[1024,1024]{1,0:T(8,128)}, s32[8,2]{0,1:T(2,128)S(1)}, f32[8,128,128]{2,1,0:T(8,128)S(1)}, s32[]{:T(128)}) while((s32[]{:T(128)}, f32[1024,1024]{1,0:T(8,128)}, s32[8,2]{0,1:T(2,128)S(1)}, f32[8,128,128]{2,1,0:T(8,128)S(1)}, s32[]{:T(128)}) %tuple.131), condition=%wide.while_cond, body=%wide.while_body.sunk | while | flops 2 | bytes 131189 | solution.py:26
  102.0 2.3 bitcast_dynamic-update-slice_fusion.4
  108.0 2.3 bitcast_dynamic-update-slice_fusion.4
  111.1 2.3 bitcast_dynamic-update-slice_fusion.4
  114.1 2.3 bitcast_dynamic-update-slice_fusion.4
  117.1 2.3 bitcast_dynamic-update-slice_fusion.4
  122.4 78.6 %custom-call.4 = f32[8,128,128]{1,2,0:T(8,128)S(1)} custom-call(f32[8,128,128]{2,1,0:T(8,128)S(1)} %get-tuple-element.17), custom_call_target="InvertDiagBlocksLowerTriangular" | custom-call | tf_op jit(solution)/shard_map/jit(_solve_triangular)/triangular_solve | solution.py:26
  212.5 4.8 bitcast_select_fusion
  217.2 43.9 %all-gather.12.cloned.1.call-done = f32[1024,1024]{0,1:T(8,128)} async-done(((f32[1024,32]{0,1:T(8,128)}), f32[1024,1024]{0,1:T(8,128)}) %all-gather.12.cloned.1.call-update) | async-done | bytes 4194320 | tf_op jit(solution)/shard_map/all_gather | solution.py:27
  261.2 17.2 %fusion.78 = f32[1056,1024]{1,0:T(8,128)S(1)} fusion(f32[1056,1024]{1,0:T(8,128)} %all-gather.14.cloned.1.call-done, f32[1024,1024]{0,1:T(8,128)} %all-gather.12.cloned.1.call-done), kind=kOutput, calls=%fused_computation.199 | convolution fusion | flops 13287555072 | bytes 12845056 | tf_op jit(solution)/shard_map/dot_general | solution.py:31
  280.4 5.3 slice_subtract_fusion.1
  286.8 5.2 all-to-all-start.1
  292.2 22.5 %while.5 = (s32[]{:T(128)}, f32[1024,1024]{1,0:T(8,128)}, s32[8,2]{0,1:T(2,128)S(1)}, f32[8,128,128]{2,1,0:T(8,128)S(1)}, s32[]{:T(128)}) while((s32[]{:T(128)}, f32[1024,1024]{1,0:T(8,128)}, s32[8,2]{0,1:T(2,128)S(1)}, f32[8,128,128]{2,1,0:T(8,128)S(1)}, s32[]{:T(128)}) %tuple.149), condition=%wide.while_cond.clone, body=%wide.while_body.clone.sunk | while | flops 2 | bytes 131189 | solution.py:26
  314.7 78.6 %custom-call.5 = f32[8,128,128]{1,2,0:T(8,128)S(1)} custom-call(f32[8,128,128]{2,1,0:T(8,128)S(1)} %get-tuple-element.18), custom_call_target="InvertDiagBlocksLowerTriangular" | custom-call | tf_op jit(solution)/shard_map/jit(_solve_triangular)/triangular_solve | solution.py:26
  407.0 52.2 %all-gather.16.cloned.1.call-done = f32[1024,1024]{0,1:T(8,128)} async-done(((f32[1024,32]{0,1:T(8,128)}), f32[1024,1024]{0,1:T(8,128)}) %all-gather.16.cloned.1.call-update) | async-done | bytes 4194320 | tf_op jit(solution)/shard_map/all_gather | solution.py:27
  461.8 62.9 %all-gather.22.cloned.1.call-done = f32[1024,1,1024]{2,0,1:T(8,128)} async-done(((f32[1024,1,128]{2,0,1:T(8,128)}), f32[1024,1,1024]{2,0,1:T(8,128)}) %all-gather.22.cloned.1.call-update) | async-done | bytes 4194320 | tf_op jit(solution)/shard_map/all_gather | solution.py:32
  524.8 29.4 %fusion = f32[1024,1024]{1,0:T(8,128)} fusion(f32[1056,1024]{1,0:T(8,128)} %copy-done.6, f32[]{:T(128)} %bitcast.17, f32[1024]{0:T(1024)S(1)} %bitcast.236, f32[1024]{0:T(1024)S(1)} %bitcast.243, f32[]{:T(128)} %bitcast.15, f32[1024]{0:T(1024)S(1)} %bitcast.234, f32[1024]{0:T(1024)S(1)} %bitcast.244, f32[]{:T(128)} %bitcast.13, f32[1024]{0:T(1024)S(1)} %bitcast.232, ...), kind=kOutput, calls=%fused_computation.5 | convolution fusion | flops 12926844928 | bytes 16842784 | tf_op jit(solution)/shard_map/dot_general | solution.py:31
  (139 shorter events, 71.8 us)
Async XLA Ops:
  7.2 60.3 %copy-start.2 = (f32[8,1024]{1,0:T(8,128)S(1)}, f32[8,1024]{1,0:T(8,128)}, u32[]{:S(2)}) copy-start(f32[8,1024]{1,0:T(8,128)} %param.10) | copy-start | bytes 98308
  7.2 60.4 %copy-start.5 = (f32[8,2,32]{2,1,0:T(2,128)S(1)}, f32[8,2,32]{2,1,0:T(2,128)}, u32[]{:S(2)}) copy-start(f32[8,2,32]{2,1,0:T(2,128)} %param.8) | copy-start | bytes 6148
  7.2 60.5 %copy-start.4 = (f32[8]{0:T(128)S(1)}, f32[8]{0:T(128)}, u32[]{:S(2)}) copy-start(f32[8]{0:T(128)} %param.11) | copy-start | bytes 100
  7.2 86.3 %all-gather.18.cloned.1.call-start = ((), (), s32[]{:S(2)}) async-start(), calls=%async_computation.5 | async-start | bytes 4325376 | tf_op jit(solution)/shard_map/all_gather | solution.py:20
  36.6 175.9 %all-gather.20.cloned.1.call-start = ((), (), s32[]{:S(2)}) async-start(), calls=%async_computation.6 | async-start | bytes 4325376 | tf_op jit(solution)/shard_map/all_gather | solution.py:20
  63.3 154.0 %all-gather.14.cloned.1.call-start = ((), (), s32[]{:S(2)}) async-start(), calls=%async_computation.3 | async-start | bytes 4866048 | tf_op jit(solution)/shard_map/all_gather | solution.py:32
  76.0 15.1 %all-to-all-start = ((f32[32,1,1024]{2,1,0:T(1,128)}), f32[32,1,1024]{2,1,0:T(1,128)S(1)}, u32[]{:S(2)}, u32[]{:S(2)}) async-start(f32[32,1,1024]{2,1,0:T(1,128)} %reshape.231), calls=%async_computation | async-start | bytes 262144 | tf_op jit(solution)/shard_map/all_to_all | solution.py:25
  83.4 177.8 %all-gather.12.cloned.1.call-start = ((), (), s32[]{:S(2)}) async-start(), calls=%async_computation.2 | async-start | bytes 4325376 | tf_op jit(solution)/shard_map/all_gather | solution.py:27
  211.8 0.7 copy-start
  278.4 2.0 copy-start.6
  286.8 106.4 %all-to-all-start.1 = ((f32[32,1,1024]{2,1,0:T(1,128)}), f32[32,1,1024]{2,1,0:T(1,128)S(1)}, u32[]{:S(2)}, u32[]{:S(2)}) async-start(f32[32,1,1024]{2,1,0:T(1,128)} %reshape.233), calls=%async_computation.1 | async-start | bytes 262144 | tf_op jit(solution)/shard_map/all_to_all | solution.py:25
  292.1 167.1 %all-gather.16.cloned.1.call-start = ((), (), s32[]{:S(2)}) async-start(), calls=%async_computation.4 | async-start | bytes 4325376 | tf_op jit(solution)/shard_map/all_gather | solution.py:27
  314.7 92.3 %copy-start.3 = (f32[8,1024]{1,0:T(8,128)S(1)}, f32[8,1024]{1,0:T(8,128)}, u32[]{:S(2)}) copy-start(f32[8,1024]{1,0:T(8,128)} %param.9) | copy-start | bytes 98308
  405.7 0.7 copy-start.1
  406.4 118.4 %all-gather.22.cloned.1.call-start = ((), (), s32[]{:S(2)}) async-start(), calls=%async_computation.7 | async-start | bytes 4718592 | tf_op jit(solution)/shard_map/all_gather | solution.py:32
Sparse Core Ops, SparseCore 0:
  36.7 50.4 all-gather.17
  89.8 51.4 all-gather.19
  143.1 63.5 all-gather.13
  212.6 48.5 all-gather.11
  406.5 52.6 all-gather.15
  460.8 63.9 all-gather.21
where the time goes:
time: 563 us; the launch traced here: 561 us
  other arithmetic  182 us (32%)
  waiting for transfers between devices  167 us (30%)
  matrix products  67.7 us (12%)
  local copies, waits for them, and re-layouts  61.2 us (11%)
  blocking collectives  55 us (10%)
  between operations  14.6 us (3%)
  starting transfers between devices  12.8 us (2%)
    another operation x5, other arithmetic, solve_panel(): jax.scipy.linalg.solve_triangular(triangle, spread, lower=True)  167 us
    all_gather x2, waiting for transfers between devices, solve_panel(): return lax.all_gather(partial_value, 'row', axis=1, tiled=True)  96.1 us
    all_gather x2, waiting for transfers between devices, apply_panel(): lax.all_gather(rows_factor, 'col', axis=1, tiled=True)  62.9 us
    all_gather x2, blocking collectives, whole_triangle(): band = lax.all_gather(block, 'col', axis=1, tiled=True)  55 us
    dot_general x2, matrix products, apply_panel(): jnp.dot(lax.all_gather(rows_factor, 'col', axis=1, tiled=True), solved, p...  46.5 us
    another operation x51, local copies, waits for them, and re-layouts, solve_panel(): jax.scipy.linalg.solve_triangular(triangle, spread, lower=True)  46.4 us
    another operation x30, matrix products, solve_panel(): jax.scipy.linalg.solve_triangular(triangle, spread, lower=True)  21.2 us
    all_to_all x2, starting transfers between devices, solve_panel(): lax.all_to_all(right_side, 'row', split_axis=1, concat_axis=0, tiled=True)  12.6 us
  transfers between devices with their start and end apart: 8, of which 4 were waited for; matrix products, arithmetic and copies ran while one was open for 43% of the time, Pallas kernels for 0%

commit v1 on v0

--- a/solution.py
+++ b/solution.py
@@ -24,7 +24,9 @@
     triangle = whole_triangle(block)
     spread = lax.all_to_all(right_side, "row", split_axis=1, concat_axis=0, tiled=True)
     partial_value = jax.scipy.linalg.solve_triangular(triangle, spread, lower=True)
-    return lax.all_gather(partial_value, "row", axis=1, tiled=True)
+    return jnp.concatenate(
+        lax.all_to_all(jnp.stack([partial_value] * lax.axis_size("row")), "row", 0, 0), axis=1
+    )
 
 
 def apply_panel(rows_factor, solved):

time: 563 us -> 528 us (0.938)
  the two profiles are of different devices: /device:TPU:0 before, /device:TPU:32 now
where the time goes in v1:
time: 528 us; the launch traced here: 518 us
  other arithmetic  181 us (34%)
  waiting for transfers between devices  94.8 us (18%)
  local copies, waits for them, and re-layouts  68.8 us (13%)
  matrix products  67.5 us (13%)
  blocking collectives  56 us (11%)
  starting transfers between devices  34.9 us (7%)
  between operations  14.6 us (3%)
    another operation x5, other arithmetic, solve_panel(): jax.scipy.linalg.solve_triangular(triangle, spread, lower=True)  167 us
    all_to_all x2, waiting for transfers between devices, solve_panel(): lax.all_to_all(jnp.stack([partial_value] * lax.axis_size('row')), 'row',...  91.1 us
    all_gather x2, blocking collectives, whole_triangle(): band = lax.all_gather(block, 'col', axis=1, tiled=True)  56 us
    another operation x51, local copies, waits for them, and re-layouts, solve_panel(): jax.scipy.linalg.solve_triangular(triangle, spread, lower=True)  47.3 us
    dot_general x2, matrix products, apply_panel(): jnp.dot(lax.all_gather(rows_factor, 'col', axis=1, tiled=True), solved, p...  46.3 us
    another operation x30, matrix products, solve_panel(): jax.scipy.linalg.solve_triangular(triangle, spread, lower=True)  21.2 us
    all_to_all x2, starting transfers between devices, solve_panel(): lax.all_to_all(jnp.stack([partial_value] * lax.axis_size('row')), 'row',...  12.7 us
    all_to_all x2, starting transfers between devices, solve_panel(): lax.all_to_all(right_side, 'row', split_axis=1, concat_axis=0, tiled=True)  11.2 us
  transfers between devices with their start and end apart: 8, of which 3 were waited for; matrix products, arithmetic and copies ran while one was open for 55% of the time, Pallas kernels for 0%

profile of v1, /device:TPU:32, one launch (start us, length us, event | category | flops | bytes accessed | tf_op | source)
XLA Modules:
  0.0 518.3 jit_solution(17880325209548639007)
XLA Ops:
  8.1 29.4 %all-gather = f32[1,32,1,1024]{3,1,2,0:T(8,128)} all-gather(f32[1,32,1,128]{3,1,2,0:T(8,128)S(1)} %bitcast.226), channel_id=2, replica_groups=mesh['row'=32,'col'=8] {'col'}, dimensions={3}, use_global_device_ids=true | all-gather | bytes 147456 | tf_op jit(solution)/shard_map/all_gather | solution.py:19
  37.5 26.6 %all-gather.2 = f32[1,32,1,1024]{3,1,2,0:T(8,128)} all-gather(f32[1,32,1,128]{3,1,2,0:T(8,128)S(1)} %bitcast.225), channel_id=4, replica_groups=mesh['row'=32,'col'=8] {'col'}, dimensions={3}, use_global_device_ids=true | all-gather | bytes 147456 | tf_op jit(solution)/shard_map/all_gather | solution.py:19
  68.4 6.1 %fusion.77 = f32[32,32,32]{2,1,0:T(8,128)S(1)} fusion(f32[]{:T(128)} %bitcast.17, f32[32,32]{1,0:T(8,128)S(1)} %sub.446, f32[32]{0:T(128)S(1)} %get-tuple-element.124, f32[]{:T(128)} %bitcast.15, f32[32,32]{1,0:T(8,128)S(1)} %sub.441, f32[32]{0:T(128)S(1)} %get-tuple-element.125, f32[]{:T(128)} %bitcast.13, f32[32,32]{1,0:T(8,128)S(1)} %sub.436, ...), kind=kLoop, calls=%fused_computation.196 | loop fusion | flops 1245184 | bytes 164896
  75.5 7.3 %all-to-all-start = ((f32[32,1,1024]{2,1,0:T(1,128)}), f32[32,1,1024]{2,1,0:T(1,128)S(1)}, u32[]{:S(2)}, u32[]{:S(2)}) async-start(f32[32,1,1024]{2,1,0:T(1,128)} %reshape.251), calls=%async_computation | async-start | bytes 262144 | tf_op jit(solution)/shard_map/all_to_all | solution.py:25
  82.9 3.3 fusion.73
  87.1 3.5 all-to-all-done
  92.9 4.8 bitcast_select_fusion.1
  97.7 24.2 %while.4 = (s32[]{:T(128)}, f32[1024,1024]{1,0:T(8,128)}, s32[8,2]{0,1:T(2,128)S(1)}, f32[8,128,128]{2,1,0:T(8,128)S(1)}, s32[]{:T(128)}) while((s32[]{:T(128)}, f32[1024,1024]{1,0:T(8,128)}, s32[8,2]{0,1:T(2,128)S(1)}, f32[8,128,128]{2,1,0:T(8,128)S(1)}, s32[]{:T(128)}) %tuple.131), condition=%wide.while_cond, body=%wide.while_body.sunk | while | flops 2 | bytes 131189 | solution.py:26
  101.4 2.3 bitcast_dynamic-update-slice_fusion.4
  121.9 78.6 %custom-call.4 = f32[8,128,128]{1,2,0:T(8,128)S(1)} custom-call(f32[8,128,128]{2,1,0:T(8,128)S(1)} %get-tuple-element.17), custom_call_target="InvertDiagBlocksLowerTriangular" | custom-call | tf_op jit(solution)/shard_map/jit(_solve_triangular)/triangular_solve | solution.py:26
  211.2 2.5 stack.10
  213.8 4.9 all-to-all-start.1
  218.7 10.9 %all-gather.16.cloned.1.call-start = ((), (), s32[]{:S(2)}) async-start(), calls=%async_computation.7 | async-start | bytes 4718592 | tf_op jit(solution)/shard_map/all_gather | solution.py:34
  229.6 4.7 bitcast_select_fusion
  234.3 37.9 %all-to-all-done.1 = f32[32,1024,32]{1,2,0:T(8,128)} async-done(((f32[32,1024,32]{1,2,0:T(8,128)}), f32[32,1024,32]{1,2,0:T(8,128)}, u32[]{:S(2)}, u32[]{:S(2)}) %all-to-all-start.1) | async-done | bytes 4194336 | tf_op jit(solution)/shard_map/all_to_all | solution.py:28
  272.1 17.2 %fusion.78 = f32[1056,1024]{1,0:T(8,128)S(1)} fusion(f32[1056,1024]{1,0:T(8,128)} %all-gather.10.cloned.1.call-done, f32[1024,1024]{0,1:T(8,128)} %bitcast.27), kind=kOutput, calls=%fused_computation.199 | convolution fusion | flops 13287555072 | bytes 12845056 | tf_op jit(solution)/shard_map/dot_general | solution.py:33
  291.3 5.3 %slice_subtract_fusion.1 = f32[32,1024]{1,0:T(8,128)S(1)} fusion(f32[1056,1024]{1,0:T(8,128)S(1)} %fusion.78, f32[]{:T(128)} %bitcast.17, f32[1024]{0:T(1024)S(1)} %bitcast.241, f32[32]{0:T(128)S(1)} %get-tuple-element.132, f32[]{:T(128)} %bitcast.15, f32[1024]{0:T(1024)S(1)} %bitcast.239, f32[32]{0:T(128)S(1)} %get-tuple-element.133, f32[]{:T(128)} %bitcast.13, ...), kind=kLoop, calls=%fused_computation.41 | loop fusion | flops 1277952 | bytes 295968 | tf_op jit(solution)/shard_map/sub | solution.py:50
  297.7 3.9 all-to-all-start.2
  301.6 23.4 %while.5 = (s32[]{:T(128)}, f32[1024,1024]{1,0:T(8,128)}, s32[8,2]{0,1:T(2,128)S(1)}, f32[8,128,128]{2,1,0:T(8,128)S(1)}, s32[]{:T(128)}) while((s32[]{:T(128)}, f32[1024,1024]{1,0:T(8,128)}, s32[8,2]{0,1:T(2,128)S(1)}, f32[8,128,128]{2,1,0:T(8,128)S(1)}, s32[]{:T(128)}) %tuple.145), condition=%wide.while_cond.clone, body=%wide.while_body.clone.sunk | while | flops 2 | bytes 131189 | solution.py:26
  325.0 78.6 %custom-call.5 = f32[8,128,128]{1,2,0:T(8,128)S(1)} custom-call(f32[8,128,128]{2,1,0:T(8,128)S(1)} %get-tuple-element.18), custom_call_target="InvertDiagBlocksLowerTriangular" | custom-call | tf_op jit(solution)/shard_map/jit(_solve_triangular)/triangular_solve | solution.py:26
  416.1 2.5 stack.12
  418.6 7.8 %all-to-all-start.3 = ((f32[32,1024,32]{1,2,0:T(8,128)}), f32[32,1024,32]{1,2,0:T(8,128)}, u32[]{:S(2)}, u32[]{:S(2)}) async-start(f32[32,1024,32]{1,2,0:T(8,128)} %stack.12), calls=%async_computation.3 | async-start | bytes 8388608 | tf_op jit(solution)/shard_map/all_to_all | solution.py:28
  426.5 53.2 %all-to-all-done.3 = f32[32,1024,32]{1,2,0:T(8,128)} async-done(((f32[32,1024,32]{1,2,0:T(8,128)}), f32[32,1024,32]{1,2,0:T(8,128)}, u32[]{:S(2)}, u32[]{:S(2)}) %all-to-all-start.3) | async-done | bytes 4194336 | tf_op jit(solution)/shard_map/all_to_all | solution.py:28
  482.4 29.0 %fusion = f32[1024,1024]{1,0:T(8,128)} fusion(f32[1056,1024]{1,0:T(8,128)} %copy-done.1, f32[]{:T(128)} %bitcast.17, f32[1024]{0:T(1024)S(1)} %bitcast.242, f32[1024]{0:T(1024)S(1)} %bitcast.249, f32[]{:T(128)} %bitcast.15, f32[1024]{0:T(1024)S(1)} %bitcast.240, f32[1024]{0:T(1024)S(1)} %bitcast.250, f32[]{:T(128)} %bitcast.13, f32[1024]{0:T(1024)S(1)} %bitcast.238, ...), kind=kOutput, calls=%fused_computation.5 | convolution fusion | flops 12926844928 | bytes 16842784 | tf_op jit(solution)/shard_map/dot_general | solution.py:33
  (129 shorter events, 82.9 us)
Async XLA Ops:
  7.2 85.7 %all-gather.12.cloned.1.call-start = ((), (), s32[]{:S(2)}) async-start(), calls=%async_computation.5 | async-start | bytes 4325376 | tf_op jit(solution)/shard_map/all_gather | solution.py:20
  37.5 192.1 %all-gather.14.cloned.1.call-start = ((), (), s32[]{:S(2)}) async-start(), calls=%async_computation.6 | async-start | bytes 4325376 | tf_op jit(solution)/shard_map/all_gather | solution.py:20
  75.5 15.1 %all-to-all-start = ((f32[32,1,1024]{2,1,0:T(1,128)}), f32[32,1,1024]{2,1,0:T(1,128)S(1)}, u32[]{:S(2)}, u32[]{:S(2)}) async-start(f32[32,1,1024]{2,1,0:T(1,128)} %reshape.251), calls=%async_computation | async-start | bytes 262144 | tf_op jit(solution)/shard_map/all_to_all | solution.py:25
  82.8 151.5 %all-gather.10.cloned.1.call-start = ((), (), s32[]{:S(2)}) async-start(), calls=%async_computation.4 | async-start | bytes 4866048 | tf_op jit(solution)/shard_map/all_gather | solution.py:34
  213.8 58.4 %all-to-all-start.1 = ((f32[32,1024,32]{1,2,0:T(8,128)}), f32[32,1024,32]{1,2,0:T(8,128)}, u32[]{:S(2)}, u32[]{:S(2)}) async-start(f32[32,1024,32]{1,2,0:T(8,128)} %stack.10), calls=%async_computation.1 | async-start | bytes 8388608 | tf_op jit(solution)/shard_map/all_to_all | solution.py:28
  218.7 263.7 %all-gather.16.cloned.1.call-start = ((), (), s32[]{:S(2)}) async-start(), calls=%async_computation.7 | async-start | bytes 4718592 | tf_op jit(solution)/shard_map/all_gather | solution.py:34
  289.4 2.0 copy-start.1
  297.7 105.9 %all-to-all-start.2 = ((f32[32,1,1024]{2,1,0:T(1,128)}), f32[32,1,1024]{2,1,0:T(1,128)S(1)}, u32[]{:S(2)}, u32[]{:S(2)}) async-start(f32[32,1,1024]{2,1,0:T(1,128)} %reshape.253), calls=%async_computation.2 | async-start | bytes 262144 | tf_op jit(solution)/shard_map/all_to_all | solution.py:25
  418.6 7.8 %copy-start = (f32[8,1024]{1,0:T(8,128)S(1)}, f32[8,1024]{1,0:T(8,128)}, u32[]{:S(2)}) copy-start(f32[8,1024]{1,0:T(8,128)} %param.9) | copy-start | bytes 98308
  418.6 61.1 %all-to-all-start.3 = ((f32[32,1024,32]{1,2,0:T(8,128)}), f32[32,1024,32]{1,2,0:T(8,128)}, u32[]{:S(2)}, u32[]{:S(2)}) async-start(f32[32,1024,32]{1,2,0:T(8,128)} %stack.12), calls=%async_computation.3 | async-start | bytes 8388608 | tf_op jit(solution)/shard_map/all_to_all | solution.py:28
Sparse Core Ops, SparseCore 0:
  37.6 51.3 all-gather.11
  91.6 51.5 all-gather.13
  144.9 63.2 all-gather.9
  229.7 63.1 all-gather.15
